TPU v7x, 32 devices: a whole 2x2x4 slice. The times are simulated.
32 devices in a mesh: mesh: 32 (over z, y, x, core).
Axes of the slice: x: 2, y: 2, z: 4, core: 2. Of those that a mesh axis runs over, the one named last changes fastest.
Arguments:
- states: float32 [196608, 256], P('mesh'), may hold values from -30 to 30
- inv_sqrt_mass: float32 [196608], P('mesh'), may hold values from 0.25 to 1.75
- element_blocks: bfloat16 [512, 512, 512], P('mesh'), may hold values from -0.25 to 0.25
- element_nodes: int32 [512, 512], P('mesh'), may hold values from 0 to 6143, as said below
- element_counts: int32 [32], P('mesh'), may hold values from 1 to 16, as said below
- node_counts: int32 [32], replicated, may hold values from 4608 to 6144, as said below
- boundary_rows: int32 [32, 2, 384], P('mesh'), may hold values from 0 to 4607, as said below
Outputs:
- rotated: float32 [196608, 256], P('mesh')
Inputs may be any that keep to these rules, and one draw needn't show every extreme that they name: `node_counts`: live node rows of each device; some device has 6144. `element_counts`: live element slots of each device (the first slots are live); some device has 16. `element_nodes`: every entry is below its device's node count. `boundary_rows`: for each device the 768 entries are distinct rows below 4608.
All inputs are finite; a program needn't handle non-finite values.
Results may differ from a plain program's by a relative error of at most 0.0077.
Values sent between devices are 32-bit elements; how exact they have to be, the bound alone decides.
A program may use at most 128 MiB of HBM per device.

v0:
```python
import jax
import jax.numpy as jnp
from jax import lax
from jax.sharding import PartitionSpec as P


def passed_along(block, axis, distance):
    devices = range(lax.axis_size(axis))
    route = [(i - distance, i) for i in devices if i - distance in devices]
    return lax.ppermute(block, axis, route)


def body(
    states, inv_sqrt_mass, element_blocks, element_nodes, element_counts, node_counts, boundary_rows
):
    position = lax.axis_index("mesh")
    devices = lax.axis_size("mesh")
    row_total = states.shape[0]
    width = states.shape[1]
    slots = element_blocks.shape[0]
    lower_rows = boundary_rows[0, 0]
    upper_rows = boundary_rows[0, 1]
    shared = lower_rows.shape[0]
    has_below = position >= 1
    owner_vals, owner_mass = passed_along(
        (states[upper_rows], inv_sqrt_mass[upper_rows]), "mesh", 1
    )
    field = states.at[lower_rows].set(jnp.where(has_below, owner_vals, states[lower_rows]))
    mass = inv_sqrt_mass.at[lower_rows].set(
        jnp.where(has_below, owner_mass, inv_sqrt_mass[lower_rows])
    )
    live_slots = element_counts[0]
    row_index = jnp.arange(row_total)
    slot_index = jnp.arange(slots)
    slot_live = slot_index < live_slots

    def ham(values):
        scaled = (mass[:, None] * values).astype(jnp.bfloat16)
        empty = jnp.zeros((row_total, width), jnp.float32)

        def add_element(slot, total):
            rows = element_nodes[slot]

            def compute(acc):
                part = jnp.dot(
                    element_blocks[slot], scaled[rows], preferred_element_type=jnp.float32
                )
                return acc.at[rows].add(part)

            return lax.cond(slot_live[slot], compute, lambda acc: acc, total)

        local = lax.fori_loop(0, slots, add_element, empty)
        coming_up = passed_along(local[upper_rows], "mesh", 1)
        coming_down = passed_along(local[lower_rows], "mesh", -1)
        assembled = local.at[lower_rows].add(coming_up).at[upper_rows].add(coming_down)
        return mass[:, None] * assembled

    center = 0.5
    half_width = 1.5
    first = (ham(field) - center * field) / half_width
    second = 2.0 * (ham(first) - center * first) / half_width - field
    filtered = 2.0 * (ham(second) - center * second) / half_width - first
    live = row_index < node_counts[position]
    in_lower = jnp.any(row_index[:, None] == lower_rows[None, :], axis=1)
    owned = live & jnp.logical_not(in_lower & has_below)
    weighted = jnp.where(owned[:, None], filtered, 0.0)
    partial_value = lax.dot_general(
        weighted,
        weighted,
        (((0,), (0,)), ((), ())),
        precision=lax.Precision.HIGHEST,
        preferred_element_type=jnp.float32,
    )
    gram = lax.psum(partial_value, "mesh")
    total = (jnp.sum(node_counts) - shared * (devices - 1)).astype(jnp.float32)
    gram = gram / total
    factor = jnp.linalg.cholesky(gram)
    inverse = jax.scipy.linalg.solve_triangular(
        factor, jnp.eye(width, dtype=jnp.float32), lower=True
    )
    rotated = jnp.dot(
        filtered, inverse.T, precision=lax.Precision.HIGHEST, preferred_element_type=jnp.float32
    )
    return jnp.where(live[:, None], rotated, 0.0)


def solution(mesh):
    in_specs = (
        P("mesh", None),
        P("mesh"),
        P("mesh", None, None),
        P("mesh", None),
        P("mesh"),
        P(),
        P("mesh", None, None),
    )
    out_specs = P("mesh", None)
    return jax.shard_map(body, mesh=mesh, in_specs=in_specs, out_specs=out_specs, check_vma=False)
```

profile of v0, /device:TPU:0, one launch (start us, length us, event | category | flops | bytes accessed | tf_op | source)
XLA Modules:
  0.0 1117.1 jit_solution(17529059180484307456)
XLA Ops:
  7.3 5.8 copy.66
  33.3 9.7 scatter_custom_fusion.4
  49.4 75.4 %while.49 = (s32[]{:T(128)}, f32[6144,256]{1,0:T(8,128)}, pred[16]{0:T(512)(128)(4,1)S(1)}, s32[16,512]{1,0:T(8,128)}, bf16[16,512,512]{2,1,0:T(8,128)(2,1)}, /*index=5*/bf16[6144,256]{1,0:T(8,128)(2,1)S(1)}, s32[]{:T(128)}) while((s32[]{:T(128)}, f32[6144,256]{1,0:T(8,128)}, pred[16]{0:T(512)(128)(4,1)S(1)}, s32[16,512]{1,0:T(8,128)}, ...), condition=%wide.region_6.7_spmd, body=%wide.region_2.6_spmd.sunk | while | flops 134351360 | bytes 3422386 | solution.py:52
  50.7 13.8 %conditional.6 = (f32[6144,256]{1,0:T(8,128)}) conditional(s32[]{:T(128)} %bitcast.62, f32[6144,256]{1,0:T(8,128)} %get-tuple-element.664, (s32[16,512]{1,0:T(8,128)}, s32[]{:T(128)}, bf16[16,512,512]{2,1,0:T(8,128)(2,1)}, bf16[6144,256]{1,0:T(8,128)(2,1)S(1)}, f32[6144,256]{1,0:T(8,128)}) %tuple.128), branch_computations={%region_3.3_spmd, %region_4.5_spmd} | conditional | flops 134351360 | bytes 3422258 | solution.py:50
  55.5 8.9 scatter_fusion
  65.7 13.8 %conditional.6 = (f32[6144,256]{1,0:T(8,128)}) conditional(s32[]{:T(128)} %bitcast.62, f32[6144,256]{1,0:T(8,128)} %get-tuple-element.664, (s32[16,512]{1,0:T(8,128)}, s32[]{:T(128)}, bf16[16,512,512]{2,1,0:T(8,128)(2,1)}, bf16[6144,256]{1,0:T(8,128)(2,1)S(1)}, f32[6144,256]{1,0:T(8,128)}) %tuple.128), branch_computations={%region_3.3_spmd, %region_4.5_spmd} | conditional | flops 134351360 | bytes 3422258 | solution.py:50
  70.6 8.9 scatter_fusion
  80.7 13.8 %conditional.6 = (f32[6144,256]{1,0:T(8,128)}) conditional(s32[]{:T(128)} %bitcast.62, f32[6144,256]{1,0:T(8,128)} %get-tuple-element.664, (s32[16,512]{1,0:T(8,128)}, s32[]{:T(128)}, bf16[16,512,512]{2,1,0:T(8,128)(2,1)}, bf16[6144,256]{1,0:T(8,128)(2,1)S(1)}, f32[6144,256]{1,0:T(8,128)}) %tuple.128), branch_computations={%region_3.3_spmd, %region_4.5_spmd} | conditional | flops 134351360 | bytes 3422258 | solution.py:50
  85.6 8.9 scatter_fusion
  95.7 13.8 %conditional.6 = (f32[6144,256]{1,0:T(8,128)}) conditional(s32[]{:T(128)} %bitcast.62, f32[6144,256]{1,0:T(8,128)} %get-tuple-element.664, (s32[16,512]{1,0:T(8,128)}, s32[]{:T(128)}, bf16[16,512,512]{2,1,0:T(8,128)(2,1)}, bf16[6144,256]{1,0:T(8,128)(2,1)S(1)}, f32[6144,256]{1,0:T(8,128)}) %tuple.128), branch_computations={%region_3.3_spmd, %region_4.5_spmd} | conditional | flops 134351360 | bytes 3422258 | solution.py:50
  100.6 8.9 scatter_fusion
  129.3 166.7 %collective-permute-start.2 = (f32[384,256]{1,0:T(8,128)S(1)}, f32[384,256]{1,0:T(8,128)S(1)}, u32[]{:S(2)}, u32[]{:S(2)}) collective-permute-start(f32[384,256]{1,0:T(8,128)S(1)} %gather_fusion.6), channel_id=1, source_target_pairs={{0,1},{1,2},{2,3},{3,4},{4,5},{5,6},{6,7},{7,8},{8,9},{9,10},{10,1... | collective-permute-start | bytes 1179656 | tf_op jit(solution)/shard_map/ppermute | solution.py:10
  302.3 7.8 scatter_fusion.4
  310.1 7.8 scatter_fusion.5
  318.0 5.8 multiply_convert_fusion.1
  326.9 75.4 %while.50 = (s32[]{:T(128)}, f32[6144,256]{1,0:T(8,128)}, pred[16]{0:T(512)(128)(4,1)S(1)}, s32[16,512]{1,0:T(8,128)}, bf16[16,512,512]{2,1,0:T(8,128)(2,1)}, /*index=5*/bf16[6144,256]{1,0:T(8,128)(2,1)S(1)}, s32[]{:T(128)}) while((s32[]{:T(128)}, f32[6144,256]{1,0:T(8,128)}, pred[16]{0:T(512)(128)(4,1)S(1)}, s32[16,512]{1,0:T(8,128)}, ...), condition=%wide.region_13.14_spmd, body=%wide.region_9.13_spmd.sunk | while | flops 134351360 | bytes 3422386 | solution.py:52
  328.1 13.8 %conditional.7 = (f32[6144,256]{1,0:T(8,128)}) conditional(s32[]{:T(128)} %bitcast.63, f32[6144,256]{1,0:T(8,128)} %get-tuple-element.685, (s32[16,512]{1,0:T(8,128)}, s32[]{:T(128)}, bf16[16,512,512]{2,1,0:T(8,128)(2,1)}, bf16[6144,256]{1,0:T(8,128)(2,1)S(1)}, f32[6144,256]{1,0:T(8,128)}) %tuple.130), branch_computations={%region_10.10_spmd, %region_11.12_spmd} | conditional | flops 134351360 | bytes 3422258 | solution.py:50
  333.0 8.9 scatter_fusion.1
  343.1 13.8 %conditional.7 = (f32[6144,256]{1,0:T(8,128)}) conditional(s32[]{:T(128)} %bitcast.63, f32[6144,256]{1,0:T(8,128)} %get-tuple-element.685, (s32[16,512]{1,0:T(8,128)}, s32[]{:T(128)}, bf16[16,512,512]{2,1,0:T(8,128)(2,1)}, bf16[6144,256]{1,0:T(8,128)(2,1)S(1)}, f32[6144,256]{1,0:T(8,128)}) %tuple.130), branch_computations={%region_10.10_spmd, %region_11.12_spmd} | conditional | flops 134351360 | bytes 3422258 | solution.py:50
  348.0 8.9 scatter_fusion.1
  358.1 13.8 %conditional.7 = (f32[6144,256]{1,0:T(8,128)}) conditional(s32[]{:T(128)} %bitcast.63, f32[6144,256]{1,0:T(8,128)} %get-tuple-element.685, (s32[16,512]{1,0:T(8,128)}, s32[]{:T(128)}, bf16[16,512,512]{2,1,0:T(8,128)(2,1)}, bf16[6144,256]{1,0:T(8,128)(2,1)S(1)}, f32[6144,256]{1,0:T(8,128)}) %tuple.130), branch_computations={%region_10.10_spmd, %region_11.12_spmd} | conditional | flops 134351360 | bytes 3422258 | solution.py:50
  363.0 8.9 scatter_fusion.1
  373.1 13.8 %conditional.7 = (f32[6144,256]{1,0:T(8,128)}) conditional(s32[]{:T(128)} %bitcast.63, f32[6144,256]{1,0:T(8,128)} %get-tuple-element.685, (s32[16,512]{1,0:T(8,128)}, s32[]{:T(128)}, bf16[16,512,512]{2,1,0:T(8,128)(2,1)}, bf16[6144,256]{1,0:T(8,128)(2,1)S(1)}, f32[6144,256]{1,0:T(8,128)}) %tuple.130), branch_computations={%region_10.10_spmd, %region_11.12_spmd} | conditional | flops 134351360 | bytes 3422258 | solution.py:50
  378.0 8.9 scatter_fusion.1
  406.8 167.9 %collective-permute-start.4 = (f32[384,256]{1,0:T(8,128)S(1)}, f32[384,256]{1,0:T(8,128)S(1)}, u32[]{:S(2)}, u32[]{:S(2)}) collective-permute-start(f32[384,256]{1,0:T(8,128)S(1)} %gather_fusion.8), channel_id=1, source_target_pairs={{0,1},{1,2},{2,3},{3,4},{4,5},{5,6},{6,7},{7,8},{8,9},{9,10},{10,1... | collective-permute-start | bytes 1179656 | tf_op jit(solution)/shard_map/ppermute | solution.py:10
  580.5 8.0 scatter_fusion.6
  588.5 7.8 scatter_fusion.7
  596.3 7.5 multiply_convert_fusion
  606.9 75.5 %while.51 = (s32[]{:T(128)}, f32[6144,256]{1,0:T(8,128)}, pred[16]{0:T(512)(128)(4,1)S(1)}, s32[16,512]{1,0:T(8,128)}, bf16[16,512,512]{2,1,0:T(8,128)(2,1)}, /*index=5*/bf16[6144,256]{1,0:T(8,128)(2,1)S(1)}, s32[]{:T(128)}) while((s32[]{:T(128)}, f32[6144,256]{1,0:T(8,128)}, pred[16]{0:T(512)(128)(4,1)S(1)}, s32[16,512]{1,0:T(8,128)}, ...), condition=%wide.region_20.21_spmd, body=%wide.region_16.20_spmd.sunk | while | flops 134351360 | bytes 3422386 | solution.py:52
  608.1 13.8 %conditional.8 = (f32[6144,256]{1,0:T(8,128)}) conditional(s32[]{:T(128)} %bitcast.64, f32[6144,256]{1,0:T(8,128)} %get-tuple-element.706, (s32[16,512]{1,0:T(8,128)}, s32[]{:T(128)}, bf16[16,512,512]{2,1,0:T(8,128)(2,1)}, bf16[6144,256]{1,0:T(8,128)(2,1)S(1)}, f32[6144,256]{1,0:T(8,128)}) %tuple.132), branch_computations={%region_17.17_spmd, %region_18.19_spmd} | conditional | flops 134351360 | bytes 3422258 | solution.py:50
  613.0 9.0 scatter_fusion.2
  623.2 13.8 %conditional.8 = (f32[6144,256]{1,0:T(8,128)}) conditional(s32[]{:T(128)} %bitcast.64, f32[6144,256]{1,0:T(8,128)} %get-tuple-element.706, (s32[16,512]{1,0:T(8,128)}, s32[]{:T(128)}, bf16[16,512,512]{2,1,0:T(8,128)(2,1)}, bf16[6144,256]{1,0:T(8,128)(2,1)S(1)}, f32[6144,256]{1,0:T(8,128)}) %tuple.132), branch_computations={%region_17.17_spmd, %region_18.19_spmd} | conditional | flops 134351360 | bytes 3422258 | solution.py:50
  628.0 9.0 scatter_fusion.2
  638.2 13.8 %conditional.8 = (f32[6144,256]{1,0:T(8,128)}) conditional(s32[]{:T(128)} %bitcast.64, f32[6144,256]{1,0:T(8,128)} %get-tuple-element.706, (s32[16,512]{1,0:T(8,128)}, s32[]{:T(128)}, bf16[16,512,512]{2,1,0:T(8,128)(2,1)}, bf16[6144,256]{1,0:T(8,128)(2,1)S(1)}, f32[6144,256]{1,0:T(8,128)}) %tuple.132), branch_computations={%region_17.17_spmd, %region_18.19_spmd} | conditional | flops 134351360 | bytes 3422258 | solution.py:50
  643.1 9.0 scatter_fusion.2
  653.3 13.8 %conditional.8 = (f32[6144,256]{1,0:T(8,128)}) conditional(s32[]{:T(128)} %bitcast.64, f32[6144,256]{1,0:T(8,128)} %get-tuple-element.706, (s32[16,512]{1,0:T(8,128)}, s32[]{:T(128)}, bf16[16,512,512]{2,1,0:T(8,128)(2,1)}, bf16[6144,256]{1,0:T(8,128)(2,1)S(1)}, f32[6144,256]{1,0:T(8,128)}) %tuple.132), branch_computations={%region_17.17_spmd, %region_18.19_spmd} | conditional | flops 134351360 | bytes 3422258 | solution.py:50
  658.1 9.0 scatter_fusion.2
  691.4 168.4 %collective-permute-start.6 = (f32[384,256]{1,0:T(8,128)S(1)}, f32[384,256]{1,0:T(8,128)S(1)}, u32[]{:S(2)}, u32[]{:S(2)}) collective-permute-start(f32[384,256]{1,0:T(8,128)S(1)} %gather_fusion.10), channel_id=1, source_target_pairs={{0,1},{1,2},{2,3},{3,4},{4,5},{5,6},{6,7},{7,8},{8,9},{9,10},{10,1... | collective-permute-start | bytes 1179656 | tf_op jit(solution)/shard_map/ppermute | solution.py:10
  863.8 7.9 scatter_fusion.8
  871.7 7.9 scatter_fusion.9
  879.6 9.7 multiply_subtract_fusion
  892.0 12.9 %fusion.13 = f32[256,256]{0,1:T(8,128)} fusion(f32[6144,256]{1,0:T(8,128)S(1)} %multiply_subtract_fusion, pred[6144]{0:T(1024)(128)(4,1)S(1)} %not_and_fusion), kind=kOutput, calls=%fused_computation.47 | convolution fusion | flops 4833411072 | bytes 6559744 | tf_op jit(solution)/shard_map/dot_general | solution.py:67
  906.2 132.1 %all-reduce.3.cloned.1.call-done = f32[256,256]{0,1:T(8,128)} async-done(((f32[256,256]{0,1:T(8,128)}), f32[256,256]{0,1:T(8,128)}) %all-reduce.3.cloned.1.call-update) | async-done | bytes 262160 | tf_op jit(solution)/shard_map/psum | solution.py:74
  1040.8 11.7 %cholesky.50 = f32[128,128]{1,0:T(8,128)S(1)} custom-call(f32[128,128]{1,0:T(8,128)S(1)} %cholesky.118), custom_call_target="Cholesky" | custom-call | tf_op jit(solution)/shard_map/jit(cholesky)/cholesky | solution.py:77
  1052.6 9.8 custom-call.15
  1062.8 11.7 %cholesky.105 = f32[128,128]{1,0:T(8,128)S(1)} custom-call(f32[128,128]{1,0:T(8,128)S(1)} %convolution_subtract_fusion.1), custom_call_target="Cholesky" | custom-call | tf_op jit(solution)/shard_map/jit(cholesky)/cholesky | solution.py:77
  1080.4 19.8 %custom-call.16 = f32[2,128,128]{1,2,0:T(8,128)S(1)} custom-call(f32[2,128,128]{2,1,0:T(8,128)S(1)} %get-tuple-element.459), custom_call_target="InvertDiagBlocksLowerTriangular" | custom-call | tf_op jit(solution)/shard_map/jit(_solve_triangular)/triangular_solve | solution.py:78
  1101.1 8.9 convolution_select_fusion
  (205 shorter events, 169.6 us)
Async XLA Ops:
  6.5 1031.7 %all-reduce.3.cloned.1.call-start = ((), (), s32[]{:S(2)}) async-start(), calls=%async_computation | async-start | bytes 524288 | tf_op jit(solution)/shard_map/psum | solution.py:74
  7.3 5.8 copy-start.1
  15.7 14.6 %collective-permute-start = (f32[384]{0:T(512)S(1)}, f32[384]{0:T(512)S(1)}, u32[]{:S(2)}, u32[]{:S(2)}) collective-permute-start(f32[384]{0:T(512)S(1)} %gather_fusion.3), channel_id=1, source_target_pairs={{0,1},{1,2},{2,3},{3,4},{4,5},{5,6},{6,7},{7,8},{8,9},{9,10},{10,1... | collective-permute-start | bytes 4616 | tf_op jit(solution)/shard_map/ppermute | solution.py:10
  22.5 10.8 collective-permute-start.1
  129.3 173.0 %collective-permute-start.2 = (f32[384,256]{1,0:T(8,128)S(1)}, f32[384,256]{1,0:T(8,128)S(1)}, u32[]{:S(2)}, u32[]{:S(2)}) collective-permute-start(f32[384,256]{1,0:T(8,128)S(1)} %gather_fusion.6), channel_id=1, source_target_pairs={{0,1},{1,2},{2,3},{3,4},{4,5},{5,6},{6,7},{7,8},{8,9},{9,10},{10,1... | collective-permute-start | bytes 1179656 | tf_op jit(solution)/shard_map/ppermute | solution.py:10
  300.5 9.6 collective-permute-start.3
  406.8 173.7 %collective-permute-start.4 = (f32[384,256]{1,0:T(8,128)S(1)}, f32[384,256]{1,0:T(8,128)S(1)}, u32[]{:S(2)}, u32[]{:S(2)}) collective-permute-start(f32[384,256]{1,0:T(8,128)S(1)} %gather_fusion.8), channel_id=1, source_target_pairs={{0,1},{1,2},{2,3},{3,4},{4,5},{5,6},{6,7},{7,8},{8,9},{9,10},{10,1... | collective-permute-start | bytes 1179656 | tf_op jit(solution)/shard_map/ppermute | solution.py:10
  579.1 9.3 collective-permute-start.5
  682.4 179.5 %copy-start.2 = (s32[32]{0:T(128)S(1)}, s32[32]{0:T(128)}, u32[]{:S(2)}) copy-start(s32[32]{0:T(128)} %param.24) | copy-start | bytes 388
  691.4 172.4 %collective-permute-start.6 = (f32[384,256]{1,0:T(8,128)S(1)}, f32[384,256]{1,0:T(8,128)S(1)}, u32[]{:S(2)}, u32[]{:S(2)}) collective-permute-start(f32[384,256]{1,0:T(8,128)S(1)} %gather_fusion.10), channel_id=1, source_target_pairs={{0,1},{1,2},{2,3},{3,4},{4,5},{5,6},{6,7},{7,8},{8,9},{9,10},{10,1... | collective-permute-start | bytes 1179656 | tf_op jit(solution)/shard_map/ppermute | solution.py:10
  859.7 12.0 %collective-permute-start.7 = (f32[384,256]{1,0:T(8,128)S(1)}, f32[384,256]{1,0:T(8,128)S(1)}, u32[]{:S(2)}, u32[]{:S(2)}) collective-permute-start(f32[384,256]{1,0:T(8,128)S(1)} %gather_fusion.11), channel_id=1, source_target_pairs={{1,0},{2,1},{3,2},{4,3},{5,4},{6,5},{7,6},{8,7},{9,8},{10,9},{11,1... | collective-permute-start | bytes 1179656 | tf_op jit(solution)/shard_map/ppermute | solution.py:10
  889.3 2.7 copy-start
Sparse Core Ops, SparseCore 0:
  905.0 133.2 all-reduce.2
where the time goes:
time: 1140 us; the launch traced here: 1120 us
  starting transfers between devices  514 us (45%)
  other arithmetic  258 us (23%)
  waiting for transfers between devices  132 us (12%)
  local copies, waits for them, and re-layouts  115 us (10%)
  matrix products  48.7 us (4%)
  loops' own time  32.5 us (3%)
  between operations  16.5 us (1%)
    ppermute x8, starting transfers between devices, passed_along(): return lax.ppermute(block, axis, route)  514 us
    psum x1, waiting for transfers between devices, body(): gram = lax.psum(partial_value, 'mesh')  132 us
    scatter-add x12, other arithmetic, compute(): return acc.at[rows].add(part)  107 us
    scatter-add x6, other arithmetic, ham(): local.at[lower_rows].add(coming_up).at[upper_rows].add(coming_down)  47.2 us
    another operation x6, other arithmetic, body(): factor = jnp.linalg.cholesky(gram)  34 us
    another operation x3, loops' own time, ham(): local = lax.fori_loop(0, slots, add_element, empty)  31.5 us
    dynamic_slice x48, local copies, waits for them, and re-layouts, add_element(): return lax.cond(slot_live[slot], compute, lambda acc: acc, total)  28.8 us
    dot_general x12, matrix products, compute(): jnp.dot(element_blocks[slot], scaled[rows], preferred_element_type=jnp.fl...  25.6 us
  transfers between devices with their start and end apart: 9, of which 1 were waited for; matrix products, arithmetic and copies ran while one was open for 4% of the time, Pallas kernels for 0%

commit v1 on v0

--- a/solution.py
+++ b/solution.py
@@ -71,7 +71,9 @@
         precision=lax.Precision.HIGHEST,
         preferred_element_type=jnp.float32,
     )
-    gram = lax.psum(partial_value, "mesh")
+    gram = partial_value
+    for hop in (1, 2, 4, 8, 16):
+        gram = gram + lax.ppermute(gram, "mesh", [(dev, dev ^ hop) for dev in range(32)])
     total = (jnp.sum(node_counts) - shared * (devices - 1)).astype(jnp.float32)
     gram = gram / total
     factor = jnp.linalg.cholesky(gram)

time: 1140 us -> 1030 us (0.904)
  waiting for transfers between devices: 132 us -> 31.6 us
  between operations: 16.5 us -> 3.47 us
  starting transfers between devices: 514 us -> 527 us
    psum x1 -> x0, waiting for transfers between devices: 132 us -> none  [body(): gram = lax.psum(partial_value, 'mesh')]
    ppermute x0 -> x5, waiting for transfers between devices: none -> 31.6 us  [body(): lax.ppermute(gram, 'mesh', [(dev, dev ^ hop) for dev in range(32)])]
    ppermute x0 -> x5, starting transfers between devices: none -> 13.2 us  [body(): lax.ppermute(gram, 'mesh', [(dev, dev ^ hop) for dev in range(32)])]
  transfers between devices with their start and end apart: 9 -> 13, of which waited for: 1 -> 5; matrix products, arithmetic and copies ran while one was open for 4% -> 5% of each run, Pallas kernels for 0% -> 0%
where the time goes in v1:
time: 1030 us; the launch traced here: 1010 us
  starting transfers between devices  527 us (51%)
  other arithmetic  257 us (25%)
  local copies, waits for them, and re-layouts  115 us (11%)
  matrix products  48.2 us (5%)
  loops' own time  32.5 us (3%)
  waiting for transfers between devices  31.6 us (3%)
    ppermute x8, starting transfers between devices, passed_along(): return lax.ppermute(block, axis, route)  514 us
    scatter-add x12, other arithmetic, compute(): return acc.at[rows].add(part)  107 us
    scatter-add x6, other arithmetic, ham(): local.at[lower_rows].add(coming_up).at[upper_rows].add(coming_down)  47.4 us
    another operation x6, other arithmetic, body(): factor = jnp.linalg.cholesky(gram)  34 us
    ppermute x5, waiting for transfers between devices, body(): lax.ppermute(gram, 'mesh', [(dev, dev ^ hop) for dev in range(32)])  31.6 us
    another operation x3, loops' own time, ham(): local = lax.fori_loop(0, slots, add_element, empty)  31.5 us
    dynamic_slice x48, local copies, waits for them, and re-layouts, add_element(): return lax.cond(slot_live[slot], compute, lambda acc: acc, total)  28.8 us
    dot_general x12, matrix products, compute(): jnp.dot(element_blocks[slot], scaled[rows], preferred_element_type=jnp.fl...  25.6 us
  transfers between devices with their start and end apart: 13, of which 5 were waited for; matrix products, arithmetic and copies ran while one was open for 5% of the time, Pallas kernels for 0%

profile of v1, /device:TPU:0, one launch (start us, length us, event | category | flops | bytes accessed | tf_op | source)
XLA Modules:
  0.0 1013.9 jit_solution(13592414409181475433)
XLA Ops:
  26.8 9.7 scatter_custom_fusion.4
  42.9 75.4 %while.49 = (s32[]{:T(128)}, f32[6144,256]{1,0:T(8,128)}, pred[16]{0:T(512)(128)(4,1)S(1)}, s32[16,512]{1,0:T(8,128)}, bf16[16,512,512]{2,1,0:T(8,128)(2,1)}, /*index=5*/bf16[6144,256]{1,0:T(8,128)(2,1)S(1)}, s32[]{:T(128)}) while((s32[]{:T(128)}, f32[6144,256]{1,0:T(8,128)}, pred[16]{0:T(512)(128)(4,1)S(1)}, s32[16,512]{1,0:T(8,128)}, ...), condition=%wide.region_6.7_spmd, body=%wide.region_2.6_spmd.sunk | while | flops 134351360 | bytes 3422386 | solution.py:52
  44.1 13.8 %conditional.6 = (f32[6144,256]{1,0:T(8,128)}) conditional(s32[]{:T(128)} %bitcast.62, f32[6144,256]{1,0:T(8,128)} %get-tuple-element.664, (s32[16,512]{1,0:T(8,128)}, s32[]{:T(128)}, bf16[16,512,512]{2,1,0:T(8,128)(2,1)}, bf16[6144,256]{1,0:T(8,128)(2,1)S(1)}, f32[6144,256]{1,0:T(8,128)}) %tuple.128), branch_computations={%region_3.3_spmd, %region_4.5_spmd} | conditional | flops 134351360 | bytes 3422258 | solution.py:50
  49.0 8.9 scatter_fusion
  59.2 13.8 %conditional.6 = (f32[6144,256]{1,0:T(8,128)}) conditional(s32[]{:T(128)} %bitcast.62, f32[6144,256]{1,0:T(8,128)} %get-tuple-element.664, (s32[16,512]{1,0:T(8,128)}, s32[]{:T(128)}, bf16[16,512,512]{2,1,0:T(8,128)(2,1)}, bf16[6144,256]{1,0:T(8,128)(2,1)S(1)}, f32[6144,256]{1,0:T(8,128)}) %tuple.128), branch_computations={%region_3.3_spmd, %region_4.5_spmd} | conditional | flops 134351360 | bytes 3422258 | solution.py:50
  64.0 8.9 scatter_fusion
  74.2 13.8 %conditional.6 = (f32[6144,256]{1,0:T(8,128)}) conditional(s32[]{:T(128)} %bitcast.62, f32[6144,256]{1,0:T(8,128)} %get-tuple-element.664, (s32[16,512]{1,0:T(8,128)}, s32[]{:T(128)}, bf16[16,512,512]{2,1,0:T(8,128)(2,1)}, bf16[6144,256]{1,0:T(8,128)(2,1)S(1)}, f32[6144,256]{1,0:T(8,128)}) %tuple.128), branch_computations={%region_3.3_spmd, %region_4.5_spmd} | conditional | flops 134351360 | bytes 3422258 | solution.py:50
  79.0 8.9 scatter_fusion
  89.2 13.8 %conditional.6 = (f32[6144,256]{1,0:T(8,128)}) conditional(s32[]{:T(128)} %bitcast.62, f32[6144,256]{1,0:T(8,128)} %get-tuple-element.664, (s32[16,512]{1,0:T(8,128)}, s32[]{:T(128)}, bf16[16,512,512]{2,1,0:T(8,128)(2,1)}, bf16[6144,256]{1,0:T(8,128)(2,1)S(1)}, f32[6144,256]{1,0:T(8,128)}) %tuple.128), branch_computations={%region_3.3_spmd, %region_4.5_spmd} | conditional | flops 134351360 | bytes 3422258 | solution.py:50
  94.1 8.9 scatter_fusion
  122.8 166.7 %collective-permute-start.2 = (f32[384,256]{1,0:T(8,128)S(1)}, f32[384,256]{1,0:T(8,128)S(1)}, u32[]{:S(2)}, u32[]{:S(2)}) collective-permute-start(f32[384,256]{1,0:T(8,128)S(1)} %gather_fusion.6), channel_id=1, source_target_pairs={{0,1},{1,2},{2,3},{3,4},{4,5},{5,6},{6,7},{7,8},{8,9},{9,10},{10,1... | collective-permute-start | bytes 1179656 | tf_op jit(solution)/shard_map/ppermute | solution.py:10
  295.5 7.8 scatter_fusion.4
  303.3 7.8 scatter_fusion.5
  320.0 75.4 %while.50 = (s32[]{:T(128)}, f32[6144,256]{1,0:T(8,128)}, pred[16]{0:T(512)(128)(4,1)S(1)}, s32[16,512]{1,0:T(8,128)}, bf16[16,512,512]{2,1,0:T(8,128)(2,1)}, /*index=5*/bf16[6144,256]{1,0:T(8,128)(2,1)S(1)}, s32[]{:T(128)}) while((s32[]{:T(128)}, f32[6144,256]{1,0:T(8,128)}, pred[16]{0:T(512)(128)(4,1)S(1)}, s32[16,512]{1,0:T(8,128)}, ...), condition=%wide.region_13.14_spmd, body=%wide.region_9.13_spmd.sunk | while | flops 134351360 | bytes 3422386 | solution.py:52
  321.3 13.8 %conditional.7 = (f32[6144,256]{1,0:T(8,128)}) conditional(s32[]{:T(128)} %bitcast.63, f32[6144,256]{1,0:T(8,128)} %get-tuple-element.685, (s32[16,512]{1,0:T(8,128)}, s32[]{:T(128)}, bf16[16,512,512]{2,1,0:T(8,128)(2,1)}, bf16[6144,256]{1,0:T(8,128)(2,1)S(1)}, f32[6144,256]{1,0:T(8,128)}) %tuple.130), branch_computations={%region_10.10_spmd, %region_11.12_spmd} | conditional | flops 134351360 | bytes 3422258 | solution.py:50
  326.1 8.9 scatter_fusion.1
  336.3 13.8 %conditional.7 = (f32[6144,256]{1,0:T(8,128)}) conditional(s32[]{:T(128)} %bitcast.63, f32[6144,256]{1,0:T(8,128)} %get-tuple-element.685, (s32[16,512]{1,0:T(8,128)}, s32[]{:T(128)}, bf16[16,512,512]{2,1,0:T(8,128)(2,1)}, bf16[6144,256]{1,0:T(8,128)(2,1)S(1)}, f32[6144,256]{1,0:T(8,128)}) %tuple.130), branch_computations={%region_10.10_spmd, %region_11.12_spmd} | conditional | flops 134351360 | bytes 3422258 | solution.py:50
  341.1 8.9 scatter_fusion.1
  351.3 13.8 %conditional.7 = (f32[6144,256]{1,0:T(8,128)}) conditional(s32[]{:T(128)} %bitcast.63, f32[6144,256]{1,0:T(8,128)} %get-tuple-element.685, (s32[16,512]{1,0:T(8,128)}, s32[]{:T(128)}, bf16[16,512,512]{2,1,0:T(8,128)(2,1)}, bf16[6144,256]{1,0:T(8,128)(2,1)S(1)}, f32[6144,256]{1,0:T(8,128)}) %tuple.130), branch_computations={%region_10.10_spmd, %region_11.12_spmd} | conditional | flops 134351360 | bytes 3422258 | solution.py:50
  356.2 8.9 scatter_fusion.1
  366.3 13.8 %conditional.7 = (f32[6144,256]{1,0:T(8,128)}) conditional(s32[]{:T(128)} %bitcast.63, f32[6144,256]{1,0:T(8,128)} %get-tuple-element.685, (s32[16,512]{1,0:T(8,128)}, s32[]{:T(128)}, bf16[16,512,512]{2,1,0:T(8,128)(2,1)}, bf16[6144,256]{1,0:T(8,128)(2,1)S(1)}, f32[6144,256]{1,0:T(8,128)}) %tuple.130), branch_computations={%region_10.10_spmd, %region_11.12_spmd} | conditional | flops 134351360 | bytes 3422258 | solution.py:50
  371.2 8.9 scatter_fusion.1
  399.9 167.9 %collective-permute-start.4 = (f32[384,256]{1,0:T(8,128)S(1)}, f32[384,256]{1,0:T(8,128)S(1)}, u32[]{:S(2)}, u32[]{:S(2)}) collective-permute-start(f32[384,256]{1,0:T(8,128)S(1)} %gather_fusion.8), channel_id=1, source_target_pairs={{0,1},{1,2},{2,3},{3,4},{4,5},{5,6},{6,7},{7,8},{8,9},{9,10},{10,1... | collective-permute-start | bytes 1179656 | tf_op jit(solution)/shard_map/ppermute | solution.py:10
  574.3 8.2 scatter_fusion.6
  582.5 7.8 scatter_fusion.7
  590.3 7.5 multiply_convert_fusion
  600.9 75.5 %while.51 = (s32[]{:T(128)}, f32[6144,256]{1,0:T(8,128)}, pred[16]{0:T(512)(128)(4,1)S(1)}, s32[16,512]{1,0:T(8,128)}, bf16[16,512,512]{2,1,0:T(8,128)(2,1)}, /*index=5*/bf16[6144,256]{1,0:T(8,128)(2,1)S(1)}, s32[]{:T(128)}) while((s32[]{:T(128)}, f32[6144,256]{1,0:T(8,128)}, pred[16]{0:T(512)(128)(4,1)S(1)}, s32[16,512]{1,0:T(8,128)}, ...), condition=%wide.region_20.21_spmd, body=%wide.region_16.20_spmd.sunk | while | flops 134351360 | bytes 3422386 | solution.py:52
  602.2 13.8 %conditional.8 = (f32[6144,256]{1,0:T(8,128)}) conditional(s32[]{:T(128)} %bitcast.64, f32[6144,256]{1,0:T(8,128)} %get-tuple-element.706, (s32[16,512]{1,0:T(8,128)}, s32[]{:T(128)}, bf16[16,512,512]{2,1,0:T(8,128)(2,1)}, bf16[6144,256]{1,0:T(8,128)(2,1)S(1)}, f32[6144,256]{1,0:T(8,128)}) %tuple.132), branch_computations={%region_17.17_spmd, %region_18.19_spmd} | conditional | flops 134351360 | bytes 3422258 | solution.py:50
  607.0 9.0 scatter_fusion.2
  617.2 13.8 %conditional.8 = (f32[6144,256]{1,0:T(8,128)}) conditional(s32[]{:T(128)} %bitcast.64, f32[6144,256]{1,0:T(8,128)} %get-tuple-element.706, (s32[16,512]{1,0:T(8,128)}, s32[]{:T(128)}, bf16[16,512,512]{2,1,0:T(8,128)(2,1)}, bf16[6144,256]{1,0:T(8,128)(2,1)S(1)}, f32[6144,256]{1,0:T(8,128)}) %tuple.132), branch_computations={%region_17.17_spmd, %region_18.19_spmd} | conditional | flops 134351360 | bytes 3422258 | solution.py:50
  622.1 9.0 scatter_fusion.2
  632.3 13.8 %conditional.8 = (f32[6144,256]{1,0:T(8,128)}) conditional(s32[]{:T(128)} %bitcast.64, f32[6144,256]{1,0:T(8,128)} %get-tuple-element.706, (s32[16,512]{1,0:T(8,128)}, s32[]{:T(128)}, bf16[16,512,512]{2,1,0:T(8,128)(2,1)}, bf16[6144,256]{1,0:T(8,128)(2,1)S(1)}, f32[6144,256]{1,0:T(8,128)}) %tuple.132), branch_computations={%region_17.17_spmd, %region_18.19_spmd} | conditional | flops 134351360 | bytes 3422258 | solution.py:50
  637.1 9.0 scatter_fusion.2
  647.3 13.8 %conditional.8 = (f32[6144,256]{1,0:T(8,128)}) conditional(s32[]{:T(128)} %bitcast.64, f32[6144,256]{1,0:T(8,128)} %get-tuple-element.706, (s32[16,512]{1,0:T(8,128)}, s32[]{:T(128)}, bf16[16,512,512]{2,1,0:T(8,128)(2,1)}, bf16[6144,256]{1,0:T(8,128)(2,1)S(1)}, f32[6144,256]{1,0:T(8,128)}) %tuple.132), branch_computations={%region_17.17_spmd, %region_18.19_spmd} | conditional | flops 134351360 | bytes 3422258 | solution.py:50
  652.2 9.0 scatter_fusion.2
  685.4 168.4 %collective-permute-start.6 = (f32[384,256]{1,0:T(8,128)S(1)}, f32[384,256]{1,0:T(8,128)S(1)}, u32[]{:S(2)}, u32[]{:S(2)}) collective-permute-start(f32[384,256]{1,0:T(8,128)S(1)} %gather_fusion.10), channel_id=1, source_target_pairs={{0,1},{1,2},{2,3},{3,4},{4,5},{5,6},{6,7},{7,8},{8,9},{9,10},{10,1... | collective-permute-start | bytes 1179656 | tf_op jit(solution)/shard_map/ppermute | solution.py:10
  856.6 7.9 scatter_fusion.8
  864.5 7.9 scatter_fusion.9
  872.3 9.7 multiply_subtract_fusion
  884.7 12.4 %fusion.13 = f32[256,256]{0,1:T(8,128)S(1)} fusion(f32[6144,256]{1,0:T(8,128)S(1)} %multiply_subtract_fusion, pred[6144]{0:T(1024)(128)(4,1)S(1)} %not_and_fusion), kind=kOutput, calls=%fused_computation.47 | convolution fusion | flops 4833411072 | bytes 6559744 | tf_op jit(solution)/shard_map/dot_general | solution.py:67
  909.7 7.8 collective-permute-done.10
  917.5 8.3 collective-permute-start.11
  933.1 10.9 %collective-permute-done.12 = f32[256,256]{0,1:T(8,128)S(1)} collective-permute-done((f32[256,256]{0,1:T(8,128)S(1)}, f32[256,256]{0,1:T(8,128)S(1)}, u32[]{:S(2)}, u32[]{:S(2)}) %collective-permute-start.12) | collective-permute-done | bytes 262176 | tf_op jit(solution)/shard_map/ppermute | solution.py:76
  944.2 11.7 %cholesky.50 = f32[128,128]{1,0:T(8,128)S(1)} custom-call(f32[128,128]{1,0:T(8,128)S(1)} %cholesky.118), custom_call_target="Cholesky" | custom-call | tf_op jit(solution)/shard_map/jit(cholesky)/cholesky | solution.py:79
  955.9 9.8 custom-call.15
  966.2 11.7 %cholesky.105 = f32[128,128]{1,0:T(8,128)S(1)} custom-call(f32[128,128]{1,0:T(8,128)S(1)} %convolution_subtract_fusion.1), custom_call_target="Cholesky" | custom-call | tf_op jit(solution)/shard_map/jit(cholesky)/cholesky | solution.py:79
  983.8 19.9 %custom-call.16 = f32[2,128,128]{1,2,0:T(8,128)S(1)} custom-call(f32[2,128,128]{2,1,0:T(8,128)S(1)} %get-tuple-element.459), custom_call_target="InvertDiagBlocksLowerTriangular" | custom-call | tf_op jit(solution)/shard_map/jit(_solve_triangular)/triangular_solve | solution.py:80
  1004.6 8.9 convolution_select_fusion
  (216 shorter events, 196.5 us)
Async XLA Ops:
  0.7 5.8 copy-start.1
  9.1 14.6 %collective-permute-start = (f32[384]{0:T(512)S(1)}, f32[384]{0:T(512)S(1)}, u32[]{:S(2)}, u32[]{:S(2)}) collective-permute-start(f32[384]{0:T(512)S(1)} %gather_fusion.3), channel_id=1, source_target_pairs={{0,1},{1,2},{2,3},{3,4},{4,5},{5,6},{6,7},{7,8},{8,9},{9,10},{10,1... | collective-permute-start | bytes 4616 | tf_op jit(solution)/shard_map/ppermute | solution.py:10
  16.0 10.8 %collective-permute-start.1 = (f32[384,256]{1,0:T(8,128)S(1)}, f32[384,256]{1,0:T(8,128)S(1)}, u32[]{:S(2)}, u32[]{:S(2)}) collective-permute-start(f32[384,256]{1,0:T(8,128)S(1)} %gather_fusion.5), channel_id=1, source_target_pairs={{0,1},{1,2},{2,3},{3,4},{4,5},{5,6},{6,7},{7,8},{8,9},{9,10},{10,1... | collective-permute-start | bytes 1179656 | tf_op jit(solution)/shard_map/ppermute | solution.py:10
  122.8 172.7 %collective-permute-start.2 = (f32[384,256]{1,0:T(8,128)S(1)}, f32[384,256]{1,0:T(8,128)S(1)}, u32[]{:S(2)}, u32[]{:S(2)}) collective-permute-start(f32[384,256]{1,0:T(8,128)S(1)} %gather_fusion.6), channel_id=1, source_target_pairs={{0,1},{1,2},{2,3},{3,4},{4,5},{5,6},{6,7},{7,8},{8,9},{9,10},{10,1... | collective-permute-start | bytes 1179656 | tf_op jit(solution)/shard_map/ppermute | solution.py:10
  294.0 9.3 collective-permute-start.3
  395.5 178.2 %copy-start.2 = (s32[32]{0:T(128)S(1)}, s32[32]{0:T(128)}, u32[]{:S(2)}) copy-start(s32[32]{0:T(128)} %param.24) | copy-start | bytes 388
  399.9 174.3 %collective-permute-start.4 = (f32[384,256]{1,0:T(8,128)S(1)}, f32[384,256]{1,0:T(8,128)S(1)}, u32[]{:S(2)}, u32[]{:S(2)}) collective-permute-start(f32[384,256]{1,0:T(8,128)S(1)} %gather_fusion.8), channel_id=1, source_target_pairs={{0,1},{1,2},{2,3},{3,4},{4,5},{5,6},{6,7},{7,8},{8,9},{9,10},{10,1... | collective-permute-start | bytes 1179656 | tf_op jit(solution)/shard_map/ppermute | solution.py:10
  572.3 10.2 %collective-permute-start.5 = (f32[384,256]{1,0:T(8,128)S(1)}, f32[384,256]{1,0:T(8,128)S(1)}, u32[]{:S(2)}, u32[]{:S(2)}) collective-permute-start(f32[384,256]{1,0:T(8,128)S(1)} %gather_fusion.9), channel_id=1, source_target_pairs={{1,0},{2,1},{3,2},{4,3},{5,4},{6,5},{7,6},{8,7},{9,8},{10,9},{11,1... | collective-permute-start | bytes 1179656 | tf_op jit(solution)/shard_map/ppermute | solution.py:10
  685.4 171.2 %collective-permute-start.6 = (f32[384,256]{1,0:T(8,128)S(1)}, f32[384,256]{1,0:T(8,128)S(1)}, u32[]{:S(2)}, u32[]{:S(2)}) collective-permute-start(f32[384,256]{1,0:T(8,128)S(1)} %gather_fusion.10), channel_id=1, source_target_pairs={{0,1},{1,2},{2,3},{3,4},{4,5},{5,6},{6,7},{7,8},{8,9},{9,10},{10,1... | collective-permute-start | bytes 1179656 | tf_op jit(solution)/shard_map/ppermute | solution.py:10
  853.7 10.7 %collective-permute-start.7 = (f32[384,256]{1,0:T(8,128)S(1)}, f32[384,256]{1,0:T(8,128)S(1)}, u32[]{:S(2)}, u32[]{:S(2)}) collective-permute-start(f32[384,256]{1,0:T(8,128)S(1)} %gather_fusion.11), channel_id=1, source_target_pairs={{1,0},{2,1},{3,2},{4,3},{5,4},{6,5},{7,6},{8,7},{9,8},{10,9},{11,1... | collective-permute-start | bytes 1179656 | tf_op jit(solution)/shard_map/ppermute | solution.py:10
  882.0 2.7 copy-start
  897.1 3.1 collective-permute-start.8
  900.2 9.4 collective-permute-start.9
  909.6 7.8 collective-permute-start.10
  917.5 13.5 %collective-permute-start.11 = (f32[256,256]{0,1:T(8,128)S(1)}, f32[256,256]{0,1:T(8,128)S(1)}, u32[]{:S(2)}, u32[]{:S(2)}) collective-permute-start(f32[256,256]{0,1:T(8,128)S(1)} %add.209), channel_id=1, source_target_pairs={{0,8},{1,9},{2,10},{3,11},{4,12},{5,13},{6,14},{7,15},{8,0},{9,1},... | collective-permute-start | bytes 786440 | tf_op jit(solution)/shard_map/ppermute | solution.py:76
  931.0 12.9 %collective-permute-start.12 = (f32[256,256]{0,1:T(8,128)S(1)}, f32[256,256]{0,1:T(8,128)S(1)}, u32[]{:S(2)}, u32[]{:S(2)}) collective-permute-start(f32[256,256]{0,1:T(8,128)S(1)} %add.210), channel_id=1, source_target_pairs={{0,16},{1,17},{2,18},{3,19},{4,20},{5,21},{6,22},{7,23},{8,24},{9,... | collective-permute-start | bytes 786440 | tf_op jit(solution)/shard_map/ppermute | solution.py:76
